TPU v7x, 32 devices: a whole 2x2x4 slice. The times are simulated.
32 devices in a mesh: section: 2 (over core), row: 4 (over y, x), col: 4 (over z).
Axes of the slice: x: 2, y: 2, z: 4, core: 2. Of those that a mesh axis runs over, the one named last changes fastest.
Arguments:
- out_grad: bfloat16 [2048, 256], P(('row', 'col')), may hold values from -6 to 6
- pre_act: bfloat16 [2, 2048, 256], P('section', ('row', 'col')), may hold values from -6 to 6
- aggregated: bfloat16 [2, 2048, 256], P('section', ('row', 'col')), may hold values from -6 to 6
- weights: bfloat16 [2, 256, 256], P('section'), may hold values from -0.375 to 0.375
- tiles: bfloat16 [4, 4, 64, 128, 128], P('row', 'col'), may hold values from -0.109375 to 0.109375
- tile_index: int32 [4, 4, 64, 2], P('row', 'col'), may hold values from 0 to 3, as said below
- live_count: int32 [4, 4], P('row', 'col'), may hold values from 8 to 64, as said below
Outputs:
- weight_grad: float32 [2, 256, 256], P('section')
- feature_grads: bfloat16 [2, 2048, 256], P('section', ('row', 'col'))
Inputs may be any that keep to these rules, and one draw needn't show every extreme that they name: `tile_index`: both entries index blocks of the tile: the first is under 4, the second under 4. `live_count`: some tile uses all 64 slots.
All inputs are finite; a program needn't handle non-finite values.
Results may differ from a plain program's by a relative error of at most 0.012.
Values may be sent and summed in bfloat16 or wider, within the bound.
A program may use at most 64 MiB of HBM per device.

v0:
```python
import math
import jax
import jax.numpy as jnp
from jax import lax
from jax.sharding import PartitionSpec as P


def from_behind(value, axis, steps):
    count = lax.axis_size(axis)
    leading, last = (max(0, -steps), min(count, count - steps))
    return lax.ppermute(value, axis, [(source, source + steps) for source in range(leading, last)])


def on_device(out_grad, pre_act, aggregated, weights, tiles, tile_index, live_count):
    section_id = lax.axis_index("section")
    upper = section_id == 1
    pre_layer = pre_act[0]
    saved_agg = aggregated[0]
    weight_mat = weights[0]
    tile_blocks = tiles[0, 0]
    tile_slots = tile_index[0, 0]
    tile_count = live_count[0, 0]
    node_rows = out_grad.shape[0]
    width = out_grad.shape[1]
    slot_total = tile_blocks.shape[0]
    block = tile_blocks.shape[1]
    tile_rows = node_rows * lax.axis_size("col")
    row_blocks = tile_rows // block
    group = min(32, slot_total)
    groups = slot_total // group
    grouped_slots = tile_slots.reshape(groups, group, 2)
    all_targets = jnp.arange(row_blocks, dtype=jnp.int32)

    def spread(row_grad):
        return lax.all_gather(row_grad, "row", axis=0, tiled=True)

    def block_total(source, col_blocks):
        height = source.shape[1]
        grouped_blocks = source.reshape(groups, group, height, block)

        def group_term(total, blocks_here, slots_here, first_slot):
            picked = jnp.take(col_blocks, slots_here[:, 1], axis=0)
            products = jnp.einsum(
                "sij,sjf->sif", blocks_here, picked, preferred_element_type=jnp.float32
            )
            slot_ids = first_slot + jnp.arange(group, dtype=jnp.int32)
            live = slot_ids < tile_count
            select = ((slots_here[:, 0][None, :] == all_targets[:, None]) & live[None, :]).astype(
                jnp.float32
            )
            return total + jnp.einsum("bs,sif->bif", select, products)

        start_total = jnp.zeros((row_blocks, height, width), jnp.float32)

        def scan_step(total, group_id):
            blocks_here = lax.dynamic_index_in_dim(grouped_blocks, group_id, 0, False)
            slots_here = lax.dynamic_index_in_dim(grouped_slots, group_id, 0, False)
            return (group_term(total, blocks_here, slots_here, group_id * group), None)

        total, _ = lax.scan(scan_step, start_total, jnp.arange(groups, dtype=jnp.int32))
        return total.reshape(row_blocks * height, width)

    def reduce_col(source, gathered):
        col_blocks = gathered.reshape(-1, block, width)
        height = source.shape[1]
        return lax.psum_scatter(
            block_total(source, col_blocks), "col", scatter_dimension=0, tiled=True
        )

    def local_terms(incoming):
        masked = jnp.where(pre_layer > 0, incoming, jnp.zeros_like(incoming))
        weight_term = lax.dot_general(
            saved_agg, masked, (((0,), (0,)), ((), ())), preferred_element_type=jnp.float32
        )
        row_grad = lax.dot_general(
            masked, weight_mat, (((1,), (1,)), ((), ())), preferred_element_type=jnp.float32
        ).astype(jnp.bfloat16)
        return (weight_term, row_grad)

    def backward_step(incoming):
        weight_term, row_grad = local_terms(incoming)
        summed = reduce_col(tile_blocks, spread(row_grad))
        return (weight_term, summed.astype(jnp.bfloat16))

    first_input = jnp.where(upper, out_grad, jnp.zeros_like(out_grad))
    first_weight, first_grad = backward_step(first_input)
    received = from_behind(first_grad, "section", -1)
    second_weight, second_grad = backward_step(received)
    local_weight = jnp.where(upper, first_weight, second_weight)
    feature_block = jnp.where(upper, first_grad, second_grad)
    total_weight = lax.psum(local_weight, ("row", "col"))
    node_total = node_rows * lax.axis_size("row") * lax.axis_size("col")
    weight_grad = (total_weight * (1.0 / math.sqrt(node_total)))[None]
    return (weight_grad, feature_block[None])


def solution(mesh):
    placed = (
        P(("row", "col"), None),
        P("section", ("row", "col"), None),
        P("section", ("row", "col"), None),
        P("section", None, None),
        P("row", "col", None, None, None),
        P("row", "col", None, None),
        P("row", "col"),
    )
    return jax.shard_map(
        on_device,
        mesh=mesh,
        in_specs=placed,
        out_specs=(P("section", None, None), P("section", ("row", "col"), None)),
        check_vma=False,
    )
```

profile of v0, /device:TPU:0, one launch (start us, length us, event | category | flops | bytes accessed | tf_op | source)
XLA Modules:
  0.0 212.3 jit_solution(15838875846190478118)
XLA Ops:
  7.2 0.0 copy-start
  7.2 0.0 reduce-scatter.3.cloned.1.call-start
  7.2 0.9 broadcast_compare_fusion
  8.1 0.0 copy-done
  8.1 0.2 convolution_convert_fusion.1
  8.3 10.5 %all_gather.6 = bf16[512,256]{1,0:T(8,128)(2,1)S(1)} all-gather(bf16[128,256]{1,0:T(8,128)(2,1)S(1)} %convolution_convert_fusion.1), channel_id=1, replica_groups=mesh['section'=2,'row'=4,'col'=4] {'row'}, dimensions={0}, use_global_device_ids=true | all-gather | bytes 327680 | tf_op jit(solution)/shard_map/all_gather | solution.py:35
  18.8 0.8 reshape_squeeze.7
  19.6 0.0 copy-start.2
  19.6 0.0 copy-start.3
  19.6 20.1 %while.22 = (s32[]{:T(128)}, f32[4,128,256]{2,0,1:T(4,128)S(1)}, s32[2]{0:T(128)S(1)}, s32[2,32,2]{1,2,0:T(2,128)S(1)}, s32[]{:T(128)}, /*index=5*/bf16[2,32,128...) while((s32[]{:T(128)}, f32[4,128,256]{2,0,1:T(4,128)S(1)}, ...), condition=%wide.region_1.3_spmd.clone, body=%wide.region_0.2_spmd.clone.sunk | while | flops 278136320 | bytes 12588737 | solution.py:60
  19.6 0.6 dynamic_slice.45
  22.2 2.0 gather_fusion
  24.2 2.7 %fusion.70 = bf16[32,128,256]{2,1,0:T(8,128)(2,1)S(1)} fusion(bf16[32,128,256]{2,1,0:T(8,128)(2,1)} %gather_fusion, pred[32]{0:T(512)(128)(4,1)S(1)} %get-tuple-element.273, bf16[2,32,128,128]{3,2,1,0:T(8,128)(2,1)} %get-tuple-element.310, s32[]{:T(128)S(6)} %select_n.94), kind=kOutput, calls=%fused_computation.6.clone.1 | convolution fusion | flops 269484032 | bytes 5242916 | tf_op jit(solution)/shard_map/while/body/eval_jaxpr/sij,sjf->sif/dot_general | solution.py:43
  27.6 0.7 add_compare_fusion.4
  28.2 1.4 fusion.71
  29.7 0.6 dynamic_slice.45
  32.3 2.0 gather_fusion
  34.3 2.7 %fusion.70 = bf16[32,128,256]{2,1,0:T(8,128)(2,1)S(1)} fusion(bf16[32,128,256]{2,1,0:T(8,128)(2,1)} %gather_fusion, pred[32]{0:T(512)(128)(4,1)S(1)} %get-tuple-element.273, bf16[2,32,128,128]{3,2,1,0:T(8,128)(2,1)} %get-tuple-element.310, s32[]{:T(128)S(6)} %select_n.94), kind=kOutput, calls=%fused_computation.6.clone.1 | convolution fusion | flops 269484032 | bytes 5242916 | tf_op jit(solution)/shard_map/while/body/eval_jaxpr/sij,sjf->sif/dot_general | solution.py:43
  37.6 0.7 add_compare_fusion.4
  38.3 1.4 fusion.71
  39.7 0.9 copy.10
  40.6 0.0 reduce-scatter.3.cloned.1.call-update
  40.7 0.0 all-reduce.2.cloned.1.call-start
  40.7 22.0 %reduce-scatter.3.cloned.1.call-done = f32[128,256]{1,0:T(8,128)} async-done(((f32[512,256]{1,0:T(8,128)}), f32[128,256]{1,0:T(8,128)}) %reduce-scatter.3.cloned.1.call-update) | async-done | bytes 131088 | tf_op jit(solution)/shard_map/reduce_scatter | solution.py:66
  62.7 0.9 convert_element_type.15
  63.7 1.3 collective-permute-start
  65.0 0.0 copy-done.2
  65.0 0.0 copy-done.3
  65.0 0.2 fusion.44
  65.2 1.6 collective-permute-done
  66.8 0.2 convolution_convert_fusion
  67.0 8.9 %all_gather.7 = bf16[512,256]{1,0:T(8,128)(2,1)S(1)} all-gather(bf16[128,256]{1,0:T(8,128)(2,1)S(1)} %convolution_convert_fusion), channel_id=1, replica_groups=mesh['section'=2,'row'=4,'col'=4] {'row'}, dimensions={0}, use_global_device_ids=true | all-gather | bytes 327680 | tf_op jit(solution)/shard_map/all_gather | solution.py:35
  75.9 0.9 fusion.40
  76.9 0.0 all-reduce.2.cloned.1.call-update
  76.9 0.0 reduce-scatter.5.cloned.1.call-start
  77.0 19.5 %while.23 = (s32[]{:T(128)}, f32[4,128,256]{2,0,1:T(4,128)S(1)}, s32[2]{0:T(128)S(1)}, s32[2,32,2]{1,2,0:T(2,128)S(1)}, s32[]{:T(128)}, /*index=5*/bf16[2,32,128...) while((s32[]{:T(128)}, f32[4,128,256]{2,0,1:T(4,128)S(1)}, ...), condition=%wide.region_5.7_spmd.clone, body=%wide.region_4.6_spmd.clone.sunk | while | flops 278136320 | bytes 12588737 | solution.py:60
  77.0 0.6 dynamic_slice.48
  79.3 2.0 gather_fusion.1
  81.3 2.7 %fusion.76 = bf16[32,128,256]{2,1,0:T(8,128)(2,1)S(1)} fusion(bf16[32,128,256]{2,1,0:T(8,128)(2,1)} %gather_fusion.1, pred[32]{0:T(512)(128)(4,1)S(1)} %get-tuple-element.282, bf16[2,32,128,128]{3,2,1,0:T(8,128)(2,1)} %get-tuple-element.343, s32[]{:T(128)S(6)} %select_n.96), kind=kOutput, calls=%fused_computation.28.clone.1 | convolution fusion | flops 269484032 | bytes 5242916 | tf_op jit(solution)/shard_map/while/body/eval_jaxpr/sij,sjf->sif/dot_general | solution.py:43
  84.6 0.7 add_compare_fusion.5
  85.2 1.4 fusion.77
  86.7 0.6 dynamic_slice.48
  89.0 2.0 gather_fusion.1
  91.0 2.7 %fusion.76 = bf16[32,128,256]{2,1,0:T(8,128)(2,1)S(1)} fusion(bf16[32,128,256]{2,1,0:T(8,128)(2,1)} %gather_fusion.1, pred[32]{0:T(512)(128)(4,1)S(1)} %get-tuple-element.282, bf16[2,32,128,128]{3,2,1,0:T(8,128)(2,1)} %get-tuple-element.343, s32[]{:T(128)S(6)} %select_n.96), kind=kOutput, calls=%fused_computation.28.clone.1 | convolution fusion | flops 269484032 | bytes 5242916 | tf_op jit(solution)/shard_map/while/body/eval_jaxpr/sij,sjf->sif/dot_general | solution.py:43
  94.3 0.7 add_compare_fusion.5
  95.0 1.4 fusion.77
  96.4 0.0 copy-start.1
  96.4 0.9 copy.12
  97.3 0.0 reduce-scatter.5.cloned.1.call-update
  97.3 83.9 %all-reduce.2.cloned.1.call-done = f32[256,256]{0,1:T(8,128)} async-done(((f32[256,256]{0,1:T(8,128)}), f32[256,256]{0,1:T(8,128)}) %all-reduce.2.cloned.1.call-update) | async-done | bytes 262160 | tf_op jit(solution)/shard_map/psum | solution.py:91
  181.2 1.0 multiply_bitcast_fusion
  182.2 0.8 copy.13
  183.0 21.3 %reduce-scatter.5.cloned.1.call-done = f32[128,256]{1,0:T(8,128)} async-done(((f32[512,256]{1,0:T(8,128)}), f32[128,256]{1,0:T(8,128)}) %reduce-scatter.5.cloned.1.call-update) | async-done | bytes 131088 | tf_op jit(solution)/shard_map/reduce_scatter | solution.py:66
  204.3 0.0 copy-done.1
  204.3 1.5 select_bitcast_fusion
  (21 shorter events, 0.1 us)
Async XLA Ops:
  7.2 0.9 copy-start
  7.2 55.6 %reduce-scatter.3.cloned.1.call-start = ((), (), s32[]{:S(2)}) async-start(), calls=%async_computation.2 | async-start | bytes 655360 | tf_op jit(solution)/shard_map/reduce_scatter | solution.py:66
  19.6 45.4 %copy-start.2 = (bf16[1,128,256]{2,1,0:T(8,128)(2,1)S(1)}, bf16[1,128,256]{2,1,0:T(8,128)(2,1)}, u32[]{:S(2)}) copy-start(bf16[1,128,256]{2,1,0:T(8,128)(2,1)} %param.15) | copy-start | bytes 196612
  19.6 45.4 %copy-start.3 = (bf16[128,256]{1,0:T(8,128)(2,1)S(1)}, bf16[128,256]{1,0:T(8,128)(2,1)}, u32[]{:S(2)}) copy-start(bf16[128,256]{1,0:T(8,128)(2,1)} %param.13) | copy-start | bytes 196612
  40.7 140.5 %all-reduce.2.cloned.1.call-start = ((), (), s32[]{:S(2)}) async-start(), calls=%async_computation.3 | async-start | bytes 524288 | tf_op jit(solution)/shard_map/psum | solution.py:91
  63.7 3.1 %collective-permute-start = (bf16[128,256]{1,0:T(8,128)(2,1)S(1)}, bf16[128,256]{1,0:T(8,128)(2,1)S(1)}, u32[]{:S(2)}, u32[]{:S(2)}) collective-permute-start(bf16[128,256]{1,0:T(8,128)(2,1)S(1)} %convert_element_type.15), channel_id=1, source_target_pairs={{16,0},{17,1},{18,2},{19,3},{20,4},{21,5},{22,6},{23,7},{24,8},{25... | collective-permute-start | bytes 196616 | tf_op jit(solution)/shard_map/ppermute | solution.py:11
  76.9 127.4 %reduce-scatter.5.cloned.1.call-start = ((), (), s32[]{:S(2)}) async-start(), calls=%async_computation.4 | async-start | bytes 655360 | tf_op jit(solution)/shard_map/reduce_scatter | solution.py:66
  96.4 107.9 %copy-start.1 = (f32[128,256]{1,0:T(8,128)S(1)}, f32[128,256]{1,0:T(8,128)}, u32[]{:S(2)}) copy-start(f32[128,256]{1,0:T(8,128)} %reduce-scatter.3.cloned.1.call-done) | copy-start | bytes 393220
Sparse Core Ops, SparseCore 0:
  40.8 21.9 reduce-scatter.2
  77.0 104.1 all-reduce.1
  183.6 20.6 reduce-scatter.4
where the time goes:
time: 213 us; the launch traced here: 212 us
  waiting for transfers between devices  129 us (61%)
  blocking collectives  19.4 us (9%)
  matrix products  18.1 us (8%)
  local copies, waits for them, and re-layouts  13.9 us (7%)
  between operations  13.9 us (7%)
  loops' own time  9.92 us (5%)
  other arithmetic  6.98 us (3%)
    psum x1, waiting for transfers between devices, on_device(): total_weight = lax.psum(local_weight, ('row', 'col'))  83.9 us
    reduce_scatter x2, waiting for transfers between devices, reduce_col(): lax.psum_scatter(block_total(source, col_blocks), 'col', scatter_dimensio...  43.3 us
    all_gather x2, blocking collectives, spread(): return lax.all_gather(row_grad, 'row', axis=0, tiled=True)  19.4 us
    dot_general x4, matrix products, group_term(): jnp.einsum('sij,sjf->sif', blocks_here, picked, preferred_element_type=jn...  10.8 us
    another operation x2, loops' own time, block_total(): lax.scan(scan_step, start_total, jnp.arange(groups, dtype=jnp.int32))  9.92 us
    gather x4, local copies, waits for them, and re-layouts, group_term(): picked = jnp.take(col_blocks, slots_here[:, 1], axis=0)  8.08 us
    dot_general x4, matrix products, group_term(): return total + jnp.einsum('bs,sif->bif', select, products)  5.75 us
  transfers between devices with their start and end apart: 4, of which 4 were waited for; matrix products, arithmetic and copies ran while one was open for 8% of the time, Pallas kernels for 0%

commit v1 on v0

--- a/solution.py
+++ b/solution.py
@@ -3,6 +3,18 @@
 import jax.numpy as jnp
 from jax import lax
 from jax.sharding import PartitionSpec as P
+
+
+def run_columns(packet, mesh_dim, pos_dim):
+    moved, fresh = (jax.lax.axis_size(mesh_dim), jax.lax.axis_index(mesh_dim))
+    z2, local_part = (packet, 1)
+    while local_part < moved:
+        long_array = jax.lax.ppermute(z2, mesh_dim, [(w, w ^ local_part) for w in range(moved)])
+        step_out = jnp.concatenate([z2, long_array], pos_dim)
+        res = jnp.concatenate([long_array, z2], pos_dim)
+        z2 = jnp.where(fresh & local_part == 0, step_out, res)
+        local_part = 2 * local_part
+    return z2
 
 
 def from_behind(value, axis, steps):
@@ -32,7 +44,7 @@
     all_targets = jnp.arange(row_blocks, dtype=jnp.int32)
 
     def spread(row_grad):
-        return lax.all_gather(row_grad, "row", axis=0, tiled=True)
+        return run_columns(row_grad, "row", 0)
 
     def block_total(source, col_blocks):
         height = source.shape[1]

time: 213 us -> 211 us (level)
  blocking collectives: 19.4 us -> 0 us
  waiting for transfers between devices: 129 us -> 138 us
  starting transfers between devices: 1.41 us -> 9.26 us
    all_gather x2 -> x0, blocking collectives: 19.4 us -> none  [spread(): return lax.all_gather(row_grad, 'row', axis=0, tiled=True)]
    ppermute x0 -> x4, waiting for transfers between devices: none -> 11 us  [run_columns(): jax.lax.ppermute(z2, mesh_dim, [(w, w ^ local_part) for w in range(moved)])]
    ppermute x0 -> x4, starting transfers between devices: none -> 7.85 us  [run_columns(): jax.lax.ppermute(z2, mesh_dim, [(w, w ^ local_part) for w in range(moved)])]
    psum x1, waiting for transfers between devices: 83.9 us -> 80.6 us  [on_device(): total_weight = lax.psum(local_weight, ('row', 'col'))]
  transfers between devices with their start and end apart: 4 -> 8, of which waited for: 4 -> 8; matrix products, arithmetic and copies ran while one was open for 8% -> 9% of each run, Pallas kernels for 0% -> 0%
where the time goes in v1:
time: 211 us
  waiting for transfers between devices  138 us (65%)
  matrix products  18.1 us (9%)
  local copies, waits for them, and re-layouts  14 us (7%)
  between operations  13.9 us (7%)
  loops' own time  10.5 us (5%)
  starting transfers between devices  9.26 us (4%)
  other arithmetic  7.27 us (3%)
    psum x1, waiting for transfers between devices, on_device(): total_weight = lax.psum(local_weight, ('row', 'col'))  80.6 us
    reduce_scatter x2, waiting for transfers between devices, reduce_col(): lax.psum_scatter(block_total(source, col_blocks), 'col', scatter_dimensio...  44.2 us
    ppermute x4, waiting for transfers between devices, run_columns(): jax.lax.ppermute(z2, mesh_dim, [(w, w ^ local_part) for w in range(moved)])  11 us
    dot_general x4, matrix products, group_term(): jnp.einsum('sij,sjf->sif', blocks_here, picked, preferred_element_type=jn...  10.8 us
    another operation x2, loops' own time, block_total(): lax.scan(scan_step, start_total, jnp.arange(groups, dtype=jnp.int32))  10.5 us
    gather x4, local copies, waits for them, and re-layouts, group_term(): picked = jnp.take(col_blocks, slots_here[:, 1], axis=0)  8.03 us
    ppermute x4, starting transfers between devices, run_columns(): jax.lax.ppermute(z2, mesh_dim, [(w, w ^ local_part) for w in range(moved)])  7.85 us
    dot_general x4, matrix products, group_term(): return total + jnp.einsum('bs,sif->bif', select, products)  5.75 us
  transfers between devices with their start and end apart: 8, of which 8 were waited for; matrix products, arithmetic and copies ran while one was open for 9% of the time, Pallas kernels for 0%

profile of v1, /device:TPU:0, one launch (start us, length us, event | category | flops | bytes accessed | tf_op | source)
XLA Modules:
  0.0 210.6 jit_solution(14920768915160429717)
XLA Ops:
  7.2 0.0 copy-start
  7.2 0.0 reduce-scatter.3.cloned.1.call-start
  7.2 0.9 broadcast_compare_fusion
  8.1 0.0 copy-done
  8.1 0.2 convolution_convert_fusion.1
  8.3 3.0 %collective-permute-start = (bf16[128,256]{1,0:T(8,128)(2,1)S(1)}, bf16[128,256]{1,0:T(8,128)(2,1)S(1)}, u32[]{:S(2)}, u32[]{:S(2)}) collective-permute-start(bf16[128,256]{1,0:T(8,128)(2,1)S(1)} %convolution_convert_fusion.1), channel_id=1, source_target_pairs={{0,4},{4,0},{8,12},{12,8},{1,5},{5,1},{9,13},{13,9},{2,6},{6,2},{1... | collective-permute-start | bytes 196616 | tf_op jit(solution)/shard_map/ppermute | solution.py:12
  11.3 2.9 %collective-permute-done = bf16[128,256]{1,0:T(8,128)(2,1)S(1)} collective-permute-done((bf16[128,256]{1,0:T(8,128)(2,1)S(1)}, bf16[128,256]{1,0:T(8,128)(2,1)S(1)}, u32[]{:S(2)}, u32[]{:S(2)}) %collective-permute-start) | collective-permute-done | bytes 65568 | tf_op jit(solution)/shard_map/ppermute | solution.py:12
  14.3 1.8 collective-permute-start.1
  16.1 0.8 reshape_squeeze.7
  16.9 3.0 %collective-permute-done.1 = bf16[256,256]{1,0:T(8,128)(2,1)S(1)} collective-permute-done((bf16[256,256]{1,0:T(8,128)(2,1)S(1)}, bf16[256,256]{1,0:T(8,128)(2,1)S(1)}, u32[]{:S(2)}, u32[]{:S(2)}) %collective-permute-start.1) | collective-permute-done | bytes 131104 | tf_op jit(solution)/shard_map/ppermute | solution.py:12
  19.9 0.1 maximum_select_fusion
  20.0 20.1 %while.22 = (s32[]{:T(128)}, f32[4,128,256]{2,0,1:T(4,128)S(1)}, s32[2]{0:T(128)S(1)}, s32[2,32,2]{1,2,0:T(2,128)S(1)}, s32[]{:T(128)}, /*index=5*/bf16[2,32,128...) while((s32[]{:T(128)}, f32[4,128,256]{2,0,1:T(4,128)S(1)}, ...), condition=%wide.region_1.3_spmd.clone, body=%wide.region_0.2_spmd.clone.sunk | while | flops 278136320 | bytes 12588737 | solution.py:72
  20.0 0.6 dynamic_slice.45
  22.6 2.0 gather_fusion
  24.6 2.7 %fusion.70 = bf16[32,128,256]{2,1,0:T(8,128)(2,1)S(1)} fusion(bf16[32,128,256]{2,1,0:T(8,128)(2,1)} %gather_fusion, pred[32]{0:T(512)(128)(4,1)S(1)} %get-tuple-element.273, bf16[2,32,128,128]{3,2,1,0:T(8,128)(2,1)} %get-tuple-element.310, s32[]{:T(128)S(6)} %select_n.142), kind=kOutput, calls=%fused_computation.6.clone.1 | convolution fusion | flops 269484032 | bytes 5242916 | tf_op jit(solution)/shard_map/while/body/eval_jaxpr/sij,sjf->sif/dot_general | solution.py:55
  27.9 0.7 add_compare_fusion.4
  28.6 1.4 fusion.71
  30.1 0.6 dynamic_slice.45
  32.6 2.0 gather_fusion
  34.6 2.7 %fusion.70 = bf16[32,128,256]{2,1,0:T(8,128)(2,1)S(1)} fusion(bf16[32,128,256]{2,1,0:T(8,128)(2,1)} %gather_fusion, pred[32]{0:T(512)(128)(4,1)S(1)} %get-tuple-element.273, bf16[2,32,128,128]{3,2,1,0:T(8,128)(2,1)} %get-tuple-element.310, s32[]{:T(128)S(6)} %select_n.142), kind=kOutput, calls=%fused_computation.6.clone.1 | convolution fusion | flops 269484032 | bytes 5242916 | tf_op jit(solution)/shard_map/while/body/eval_jaxpr/sij,sjf->sif/dot_general | solution.py:55
  38.0 0.7 add_compare_fusion.4
  38.7 1.4 fusion.71
  40.1 0.0 copy-start.2
  40.1 0.0 copy-start.3
  40.1 0.9 copy.10
  41.0 0.0 reduce-scatter.3.cloned.1.call-update
  41.0 0.0 all-reduce.2.cloned.1.call-start
  41.1 23.0 %reduce-scatter.3.cloned.1.call-done = f32[128,256]{1,0:T(8,128)} async-done(((f32[512,256]{1,0:T(8,128)}), f32[128,256]{1,0:T(8,128)}) %reduce-scatter.3.cloned.1.call-update) | async-done | bytes 131088 | tf_op jit(solution)/shard_map/reduce_scatter | solution.py:78
  64.1 0.9 convert_element_type.15
  65.0 1.3 collective-permute-start.2
  66.3 1.8 collective-permute-done.2
  68.1 0.2 convolution_convert_fusion
  68.3 1.5 collective-permute-start.3
  69.9 0.0 copy-done.2
  69.9 0.0 copy-done.3
  69.9 0.2 fusion.44
  70.1 2.6 %collective-permute-done.3 = bf16[128,256]{1,0:T(8,128)(2,1)S(1)} collective-permute-done((bf16[128,256]{1,0:T(8,128)(2,1)S(1)}, bf16[128,256]{1,0:T(8,128)(2,1)S(1)}, u32[]{:S(2)}, u32[]{:S(2)}) %collective-permute-start.3) | collective-permute-done | bytes 65568 | tf_op jit(solution)/shard_map/ppermute | solution.py:12
  72.7 1.5 collective-permute-start.4
  74.1 0.9 fusion.40
  75.1 0.0 all-reduce.2.cloned.1.call-update
  75.1 0.0 reduce-scatter.5.cloned.1.call-start
  75.1 2.6 %collective-permute-done.4 = bf16[256,256]{1,0:T(8,128)(2,1)S(1)} collective-permute-done((bf16[256,256]{1,0:T(8,128)(2,1)S(1)}, bf16[256,256]{1,0:T(8,128)(2,1)S(1)}, u32[]{:S(2)}, u32[]{:S(2)}) %collective-permute-start.4) | collective-permute-done | bytes 131104 | tf_op jit(solution)/shard_map/ppermute | solution.py:12
  77.7 0.1 maximum_select_fusion.1
  77.8 20.1 %while.23 = (s32[]{:T(128)}, f32[4,128,256]{2,0,1:T(4,128)S(1)}, s32[2]{0:T(128)S(1)}, s32[2,32,2]{1,2,0:T(2,128)S(1)}, s32[]{:T(128)}, /*index=5*/bf16[2,32,128...) while((s32[]{:T(128)}, f32[4,128,256]{2,0,1:T(4,128)S(1)}, ...), condition=%wide.region_5.7_spmd.clone, body=%wide.region_4.6_spmd.clone.sunk | while | flops 278136320 | bytes 12588737 | solution.py:72
  77.8 0.7 dynamic_slice.48
  80.4 2.0 gather_fusion.1
  82.4 2.7 %fusion.76 = bf16[32,128,256]{2,1,0:T(8,128)(2,1)S(1)} fusion(bf16[32,128,256]{2,1,0:T(8,128)(2,1)} %gather_fusion.1, pred[32]{0:T(512)(128)(4,1)S(1)} %get-tuple-element.282, bf16[2,32,128,128]{3,2,1,0:T(8,128)(2,1)} %get-tuple-element.343, s32[]{:T(128)S(6)} %select_n.144), kind=kOutput, calls=%fused_computation.28.clone.1 | convolution fusion | flops 269484032 | bytes 5242916 | tf_op jit(solution)/shard_map/while/body/eval_jaxpr/sij,sjf->sif/dot_general | solution.py:55
  85.8 0.7 add_compare_fusion.5
  86.5 1.4 fusion.77
  87.9 0.7 dynamic_slice.48
  90.5 2.0 gather_fusion.1
  92.5 2.7 %fusion.76 = bf16[32,128,256]{2,1,0:T(8,128)(2,1)S(1)} fusion(bf16[32,128,256]{2,1,0:T(8,128)(2,1)} %gather_fusion.1, pred[32]{0:T(512)(128)(4,1)S(1)} %get-tuple-element.282, bf16[2,32,128,128]{3,2,1,0:T(8,128)(2,1)} %get-tuple-element.343, s32[]{:T(128)S(6)} %select_n.144), kind=kOutput, calls=%fused_computation.28.clone.1 | convolution fusion | flops 269484032 | bytes 5242916 | tf_op jit(solution)/shard_map/while/body/eval_jaxpr/sij,sjf->sif/dot_general | solution.py:55
  95.9 0.7 add_compare_fusion.5
  96.5 1.4 fusion.77
  98.0 0.0 copy-start.1
  98.0 0.9 copy.12
  98.9 0.0 reduce-scatter.5.cloned.1.call-update
  98.9 80.6 %all-reduce.2.cloned.1.call-done = f32[256,256]{0,1:T(8,128)} async-done(((f32[256,256]{0,1:T(8,128)}), f32[256,256]{0,1:T(8,128)}) %all-reduce.2.cloned.1.call-update) | async-done | bytes 262160 | tf_op jit(solution)/shard_map/psum | solution.py:103
  179.5 1.0 multiply_bitcast_fusion
  180.4 0.8 copy.13
  181.3 21.3 %reduce-scatter.5.cloned.1.call-done = f32[128,256]{1,0:T(8,128)} async-done(((f32[512,256]{1,0:T(8,128)}), f32[128,256]{1,0:T(8,128)}) %reduce-scatter.5.cloned.1.call-update) | async-done | bytes 131088 | tf_op jit(solution)/shard_map/reduce_scatter | solution.py:78
  202.5 0.0 copy-done.1
  202.5 1.5 select_bitcast_fusion
  (23 shorter events, 0.2 us)
Async XLA Ops:
  7.2 1.0 copy-start
  7.2 56.9 %reduce-scatter.3.cloned.1.call-start = ((), (), s32[]{:S(2)}) async-start(), calls=%async_computation.2 | async-start | bytes 655360 | tf_op jit(solution)/shard_map/reduce_scatter | solution.py:78
  8.3 5.9 %collective-permute-start = (bf16[128,256]{1,0:T(8,128)(2,1)S(1)}, bf16[128,256]{1,0:T(8,128)(2,1)S(1)}, u32[]{:S(2)}, u32[]{:S(2)}) collective-permute-start(bf16[128,256]{1,0:T(8,128)(2,1)S(1)} %convolution_convert_fusion.1), channel_id=1, source_target_pairs={{0,4},{4,0},{8,12},{12,8},{1,5},{5,1},{9,13},{13,9},{2,6},{6,2},{1... | collective-permute-start | bytes 196616 | tf_op jit(solution)/shard_map/ppermute | solution.py:12
  14.3 5.6 %collective-permute-start.1 = (bf16[256,256]{1,0:T(8,128)(2,1)S(1)}, bf16[256,256]{1,0:T(8,128)(2,1)S(1)}, u32[]{:S(2)}, u32[]{:S(2)}) collective-permute-start(bf16[256,256]{1,0:T(8,128)(2,1)S(1)} %maximum_select_fusion.2), channel_id=1, source_target_pairs={{0,8},{4,12},{8,0},{12,4},{1,9},{5,13},{9,1},{13,5},{2,10},{6,14},... | collective-permute-start | bytes 393224 | tf_op jit(solution)/shard_map/ppermute | solution.py:12
  40.1 29.8 %copy-start.2 = (bf16[1,128,256]{2,1,0:T(8,128)(2,1)S(1)}, bf16[1,128,256]{2,1,0:T(8,128)(2,1)}, u32[]{:S(2)}) copy-start(bf16[1,128,256]{2,1,0:T(8,128)(2,1)} %param.15) | copy-start | bytes 196612
  40.1 29.7 %copy-start.3 = (bf16[128,256]{1,0:T(8,128)(2,1)S(1)}, bf16[128,256]{1,0:T(8,128)(2,1)}, u32[]{:S(2)}) copy-start(bf16[128,256]{1,0:T(8,128)(2,1)} %param.13) | copy-start | bytes 196612
  41.0 138.4 %all-reduce.2.cloned.1.call-start = ((), (), s32[]{:S(2)}) async-start(), calls=%async_computation.3 | async-start | bytes 524288 | tf_op jit(solution)/shard_map/psum | solution.py:103
  65.0 3.1 %collective-permute-start.2 = (bf16[128,256]{1,0:T(8,128)(2,1)S(1)}, bf16[128,256]{1,0:T(8,128)(2,1)S(1)}, u32[]{:S(2)}, u32[]{:S(2)}) collective-permute-start(bf16[128,256]{1,0:T(8,128)(2,1)S(1)} %convert_element_type.15), channel_id=1, source_target_pairs={{16,0},{17,1},{18,2},{19,3},{20,4},{21,5},{22,6},{23,7},{24,8},{25... | collective-permute-start | bytes 196616 | tf_op jit(solution)/shard_map/ppermute | solution.py:23
  68.3 4.3 %collective-permute-start.3 = (bf16[128,256]{1,0:T(8,128)(2,1)S(1)}, bf16[128,256]{1,0:T(8,128)(2,1)S(1)}, u32[]{:S(2)}, u32[]{:S(2)}) collective-permute-start(bf16[128,256]{1,0:T(8,128)(2,1)S(1)} %convolution_convert_fusion), channel_id=1, source_target_pairs={{0,4},{4,0},{8,12},{12,8},{1,5},{5,1},{9,13},{13,9},{2,6},{6,2},{1... | collective-permute-start | bytes 196616 | tf_op jit(solution)/shard_map/ppermute | solution.py:12
  72.7 5.0 %collective-permute-start.4 = (bf16[256,256]{1,0:T(8,128)(2,1)S(1)}, bf16[256,256]{1,0:T(8,128)(2,1)S(1)}, u32[]{:S(2)}, u32[]{:S(2)}) collective-permute-start(bf16[256,256]{1,0:T(8,128)(2,1)S(1)} %maximum_select_fusion.3), channel_id=1, source_target_pairs={{0,8},{4,12},{8,0},{12,4},{1,9},{5,13},{9,1},{13,5},{2,10},{6,14},... | collective-permute-start | bytes 393224 | tf_op jit(solution)/shard_map/ppermute | solution.py:12
  75.1 127.4 %reduce-scatter.5.cloned.1.call-start = ((), (), s32[]{:S(2)}) async-start(), calls=%async_computation.4 | async-start | bytes 655360 | tf_op jit(solution)/shard_map/reduce_scatter | solution.py:78
  98.0 104.6 %copy-start.1 = (f32[128,256]{1,0:T(8,128)S(1)}, f32[128,256]{1,0:T(8,128)}, u32[]{:S(2)}) copy-start(f32[128,256]{1,0:T(8,128)} %reduce-scatter.3.cloned.1.call-done) | copy-start | bytes 393220
Sparse Core Ops, SparseCore 0:
  41.2 22.8 reduce-scatter.2
  75.2 104.2 all-reduce.1
  181.8 20.6 reduce-scatter.4
